TPU v7x, 768 devices: a whole 4x8x12 slice. The times are simulated.
768 devices in a mesh: ctx: 64 (over y, x, core), head: 12 (over z).
Axes of the slice: x: 4, y: 8, z: 12, core: 2. Of those that a mesh axis runs over, the one named last changes fastest.
Arguments:
- query_heads: bfloat16 [16384, 48, 128], P('ctx', 'head'), may hold values from -5 to 5
- key_head: bfloat16 [16384, 6, 128], P('ctx'), may hold values from -5 to 5
- value_head: bfloat16 [16384, 6, 128], P('ctx'), may hold values from -5 to 5
- out_grad: bfloat16 [16384, 48, 128], P('ctx', 'head'), may hold values from -5 to 5
- doc_blocks: int32 [32], replicated, may hold values from 1 to 8, 128 in all
Outputs:
- query_grad: bfloat16 [16384, 48, 128], P('ctx', 'head')
- key_grad: bfloat16 [16384, 6, 128], P('ctx')
- value_grad: bfloat16 [16384, 6, 128], P('ctx')
Inputs may be any that keep to these rules, and one draw needn't show every extreme that they name: `doc_blocks`: every document has 1 to 8 blocks, together 16384 // 128 blocks, and one document has exactly 8 blocks.
All inputs are finite; a program needn't handle non-finite values.
Results may differ from a plain program's by a relative error of at most 0.025.
Values may be sent and summed in bfloat16 or wider, within the bound.
A program may use at most 32 MiB of HBM per device.

v0:
```python
import jax
import jax.numpy as jnp
from jax import lax
from jax.sharding import PartitionSpec as P

GROUP = 8
BLOCK = 128
HOPS = 4


masked_value = -1e30


def passed_along(block, axis, distance):
    devices = range(lax.axis_size(axis))
    route = [(i - distance, i) for i in devices if i - distance in devices]
    return lax.ppermute(block, axis, route)


def doc_index(positions, doc_ends):
    return jnp.sum((positions[:, None] >= doc_ends[None, :]).astype(jnp.int32), axis=1)


def contract(first_mat, second_mat):
    return jnp.einsum("ipd,jd->pij", first_mat, second_mat, preferred_element_type=jnp.float32)


def contract_rows(weights, rows):
    return jnp.einsum("pij,ipd->jd", weights, rows, preferred_element_type=jnp.float32)


def on_device(query_heads, key_head, value_head, out_grad, doc_blocks):
    shard_len = query_heads.shape[0]
    local_heads = query_heads.shape[1]
    head_width = query_heads.shape[2]
    kv_count = key_head.shape[1]
    score_scale = head_width ** (-0.5)
    own_index = lax.axis_index("ctx")
    group_index = lax.axis_index("head") * local_heads // GROUP
    doc_ends = jnp.cumsum(doc_blocks) * BLOCK
    offsets = jnp.arange(shard_len, dtype=jnp.int32)

    def shard_docs(shard_index):
        positions = shard_index * shard_len + offsets
        return (positions, doc_index(positions, doc_ends))

    own_key = lax.dynamic_index_in_dim(key_head, group_index, axis=1, keepdims=False)
    own_value = lax.dynamic_index_in_dim(value_head, group_index, axis=1, keepdims=False)
    query_pos, query_docs = shard_docs(own_index)
    key_value = jnp.stack([own_key, own_value])
    sources = [key_value]
    for offset in range(1, HOPS + 1):
        sources.append(passed_along(key_value, "ctx", offset))
    actives = []
    scores = []
    for offset in range(HOPS + 1):
        key_pos, key_docs = shard_docs(own_index - offset)
        allowed_mask = (
            (query_docs[:, None] == key_docs[None, :])
            & (key_pos[None, :] <= query_pos[:, None])
            & (key_pos[None, :] >= 0)
        )
        if offset == 0:
            active = jnp.ones((), jnp.bool_)
        else:
            active = (query_docs[0] == key_docs[-1]) & (key_pos[-1] >= 0)
        actives.append(active)
        scores.append(
            jnp.where(
                allowed_mask[None],
                contract(query_heads, sources[offset][0]) * score_scale,
                masked_value,
            )
        )
    row_max = jnp.max(scores[0], axis=2)
    for offset in range(1, HOPS + 1):
        row_max = jnp.maximum(row_max, jnp.max(scores[offset], axis=2))
    row_sum = jnp.zeros((local_heads, shard_len), jnp.float32)
    for offset in range(HOPS + 1):
        row_sum = row_sum + jnp.sum(jnp.exp(scores[offset] - row_max[:, :, None]), axis=2)
    log_norm = row_max + jnp.log(row_sum)
    probs_full = [jnp.exp(block_scores - log_norm[:, :, None]) for block_scores in scores]
    probs_low = [block_probs.astype(jnp.bfloat16) for block_probs in probs_full]
    attended = jnp.zeros((shard_len, local_heads, head_width), jnp.float32)
    for offset in range(HOPS + 1):
        weighted_probs_low = probs_low[offset]
        attended = attended + jnp.einsum(
            "pij,jd->ipd",
            weighted_probs_low,
            sources[offset][1],
            preferred_element_type=jnp.float32,
        )
    attended_low = attended.astype(jnp.bfloat16)
    out_dot = jnp.transpose(
        jnp.sum(out_grad.astype(jnp.float32) * attended_low.astype(jnp.float32), axis=2)
    )
    query_acc = jnp.zeros((shard_len, local_heads, head_width), jnp.float32)
    returned = jnp.zeros((2, shard_len, head_width), jnp.float32)
    for offset in range(HOPS + 1):
        score_probs_full = probs_full[offset]
        dprob = contract(out_grad, sources[offset][1])
        dscore = (score_probs_full * (dprob - out_dot[:, :, None])).astype(jnp.bfloat16)
        query_term = jnp.einsum(
            "pij,jd->ipd", dscore, sources[offset][0], preferred_element_type=jnp.float32
        )
        query_term, grad_pair = (
            query_term,
            jnp.stack(
                [contract_rows(dscore, query_heads), contract_rows(probs_low[offset], out_grad)]
            ),
        )
        query_acc = query_acc + query_term
        if offset == 0:
            returned = grad_pair
        else:
            returned = returned + passed_along(grad_pair, "ctx", -offset)
    group_hot = (jnp.arange(kv_count, dtype=jnp.int32) == group_index).astype(jnp.float32)
    spread = returned[:, :, None, :] * group_hot[None, None, :, None]
    summed = lax.psum(spread, "head")
    query_grad = (query_acc * score_scale).astype(jnp.bfloat16)
    key_grad = (summed[0] * score_scale).astype(jnp.bfloat16)
    value_grad = summed[1].astype(jnp.bfloat16)
    return (query_grad, key_grad, value_grad)


def solution(mesh):
    return jax.shard_map(
        on_device,
        mesh=mesh,
        in_specs=(
            P("ctx", "head", None),
            P("ctx", None, None),
            P("ctx", None, None),
            P("ctx", "head", None),
            P(),
        ),
        out_specs=(P("ctx", "head", None), P("ctx", None, None), P("ctx", None, None)),
        check_vma=False,
    )
```

profile of v0, /device:TPU:6, one launch (start us, length us, event | category | flops | bytes accessed | tf_op | source)
XLA Modules:
  0.0 198.8 jit_solution(17383510720420256537)
XLA Ops:
  7.3 0.9 dynamic-slice_bitcast_fusion
  8.2 2.8 %collective-permute-start.2 = (bf16[2,256,128]{2,1,0:T(8,128)(2,1)S(1)}, bf16[2,256,128]{2,1,0:T(8,128)(2,1)S(1)}, u32[]{:S(2)}, u32[]{:S(2)}) collective-permute-start(bf16[2,256,128]{2,1,0:T(8,128)(2,1)S(1)} %pad_maximum_fusion.4), channel_id=1, source_target_pairs={{0,36},{12,48},{24,60},{36,72},{48,84},{60,96},{72,108},{84,120},{... | collective-permute-start | bytes 393224 | tf_op jit(solution)/shard_map/ppermute | solution.py:17
  11.1 3.4 %collective-permute-start.1 = (bf16[2,256,128]{2,1,0:T(8,128)(2,1)S(1)}, bf16[2,256,128]{2,1,0:T(8,128)(2,1)S(1)}, u32[]{:S(2)}, u32[]{:S(2)}) collective-permute-start(bf16[2,256,128]{2,1,0:T(8,128)(2,1)S(1)} %pad_maximum_fusion.4), channel_id=1, source_target_pairs={{0,24},{12,36},{24,48},{36,60},{48,72},{60,84},{72,96},{84,108},{9... | collective-permute-start | bytes 393224 | tf_op jit(solution)/shard_map/ppermute | solution.py:17
  14.5 3.8 %collective-permute-start = (bf16[2,256,128]{2,1,0:T(8,128)(2,1)S(1)}, bf16[2,256,128]{2,1,0:T(8,128)(2,1)S(1)}, u32[]{:S(2)}, u32[]{:S(2)}) collective-permute-start(bf16[2,256,128]{2,1,0:T(8,128)(2,1)S(1)} %pad_maximum_fusion.4), channel_id=1, source_target_pairs={{0,12},{12,24},{24,36},{36,48},{48,60},{60,72},{72,84},{84,96},{96... | collective-permute-start | bytes 393224 | tf_op jit(solution)/shard_map/ppermute | solution.py:17
  18.3 2.8 %collective-permute-start.3 = (bf16[2,256,128]{2,1,0:T(8,128)(2,1)S(1)}, bf16[2,256,128]{2,1,0:T(8,128)(2,1)S(1)}, u32[]{:S(2)}, u32[]{:S(2)}) collective-permute-start(bf16[2,256,128]{2,1,0:T(8,128)(2,1)S(1)} %pad_maximum_fusion.4), channel_id=1, source_target_pairs={{0,48},{12,60},{24,72},{36,84},{48,96},{60,108},{72,120},{84,132},... | collective-permute-start | bytes 393224 | tf_op jit(solution)/shard_map/ppermute | solution.py:17
  21.3 0.7 copy.94
  22.3 0.7 and_and_fusion.3
  23.0 1.2 fusion.89
  24.4 0.3 fusion.87
  24.8 0.3 fusion.88
  25.1 0.3 fusion.90
  25.4 1.7 collective-permute-done.3
  27.1 0.3 fusion.86
  27.5 0.7 exponential_reduce_fusion.3
  28.3 1.2 fusion.59
  29.4 0.3 convolution_bitcast_fusion.11
  29.8 0.3 convolution_bitcast_fusion.9
  30.1 0.3 convolution_bitcast_fusion.7
  30.4 0.3 convolution_bitcast_fusion.5
  30.7 0.3 fusion.52
  31.1 0.3 fusion.49
  31.4 0.3 convolution_add_fusion.3
  31.8 0.4 fusion.35
  32.1 1.1 fusion.24
  33.3 0.3 fusion.23
  33.6 0.3 convolution_bitcast_fusion.12
  33.9 1.9 collective-permute-start.4
  35.8 0.3 fusion.22
  36.1 0.3 convolution_bitcast_fusion.10
  36.5 2.3 %collective-permute-start.5 = (f32[2,256,128]{2,1,0:T(8,128)S(1)}, f32[2,256,128]{2,1,0:T(8,128)S(1)}, u32[]{:S(2)}, u32[]{:S(2)}) collective-permute-start(f32[2,256,128]{2,1,0:T(8,128)S(1)} %pad_maximum_fusion.1), channel_id=1, source_target_pairs={{24,0},{36,12},{48,24},{60,36},{72,48},{84,60},{96,72},{108,84},{1... | collective-permute-start | bytes 786440 | tf_op jit(solution)/shard_map/ppermute | solution.py:17
  38.7 0.3 fusion.21
  39.1 0.3 convolution_bitcast_fusion.8
  39.4 3.0 %collective-permute-start.6 = (f32[2,256,128]{2,1,0:T(8,128)S(1)}, f32[2,256,128]{2,1,0:T(8,128)S(1)}, u32[]{:S(2)}, u32[]{:S(2)}) collective-permute-start(f32[2,256,128]{2,1,0:T(8,128)S(1)} %pad_maximum_fusion.2), channel_id=1, source_target_pairs={{36,0},{48,12},{60,24},{72,36},{84,48},{96,60},{108,72},{120,84},{... | collective-permute-start | bytes 786440 | tf_op jit(solution)/shard_map/ppermute | solution.py:17
  42.4 0.3 fusion.20
  42.7 0.3 convolution_bitcast_fusion.6
  43.1 1.9 collective-permute-start.7
  45.0 0.3 convolution_bitcast_fusion.14
  45.3 0.3 convolution_bitcast_fusion.13
  45.6 7.2 %collective-permute-done.5 = f32[2,256,128]{2,1,0:T(8,128)S(1)} collective-permute-done((f32[2,256,128]{2,1,0:T(8,128)S(1)}, f32[2,256,128]{2,1,0:T(8,128)S(1)}, u32[]{:S(2)}, u32[]{:S(2)}) %collective-permute-start.5) | collective-permute-done | bytes 262176 | tf_op jit(solution)/shard_map/ppermute | solution.py:17
  52.8 5.2 %collective-permute-done.6 = f32[2,256,128]{2,1,0:T(8,128)S(1)} collective-permute-done((f32[2,256,128]{2,1,0:T(8,128)S(1)}, f32[2,256,128]{2,1,0:T(8,128)S(1)}, u32[]{:S(2)}, u32[]{:S(2)}) %collective-permute-start.6) | collective-permute-done | bytes 262176 | tf_op jit(solution)/shard_map/ppermute | solution.py:17
  58.0 2.5 %collective-permute-done.7 = f32[2,256,128]{2,1,0:T(8,128)S(1)} collective-permute-done((f32[2,256,128]{2,1,0:T(8,128)S(1)}, f32[2,256,128]{2,1,0:T(8,128)S(1)}, u32[]{:S(2)}, u32[]{:S(2)}) %collective-permute-start.7) | collective-permute-done | bytes 262176 | tf_op jit(solution)/shard_map/ppermute | solution.py:17
  60.6 1.3 broadcast_multiply_fusion
  62.0 1.2 fusion.62
  64.0 0.3 fusion.36
  64.3 0.9 copy.136
  65.1 122.9 %all-reduce.2.cloned.1.call-done = f32[2,256,6,128]{3,1,2,0:T(8,128)} async-done(((f32[2,256,6,128]{3,1,2,0:T(8,128)}), f32[2,256,6,128]{3,1,2,0:T(8,128)}) %all-reduce.2.cloned.1.call-update) | async-done | bytes 1572880 | tf_op jit(solution)/shard_map/psum | solution.py:119
  188.0 2.0 fusion.43
  190.0 1.9 fusion.44
  (46 shorter events, 1.5 us)
Async XLA Ops:
  7.2 15.9 %copy-start = (bf16[256,4,128]{2,1,0:T(4,128)(2,1)S(1)}, bf16[256,4,128]{2,1,0:T(4,128)(2,1)}, u32[]{:S(2)}) copy-start(bf16[256,4,128]{2,1,0:T(4,128)(2,1)} %param.5) | copy-start | bytes 786436
  7.2 17.0 %copy-start.8 = (bf16[256,4,128]{2,1,0:T(4,128)(2,1)S(1)}, bf16[256,4,128]{2,1,0:T(4,128)(2,1)}, u32[]{:S(2)}) copy-start(bf16[256,4,128]{2,1,0:T(4,128)(2,1)} %param.8) | copy-start | bytes 786436
  7.2 180.8 %all-reduce.2.cloned.1.call-start = ((), (), s32[]{:S(2)}) async-start(), calls=%async_computation | async-start | bytes 3145728 | tf_op jit(solution)/shard_map/psum | solution.py:119
  8.2 16.2 %collective-permute-start.2 = (bf16[2,256,128]{2,1,0:T(8,128)(2,1)S(1)}, bf16[2,256,128]{2,1,0:T(8,128)(2,1)S(1)}, u32[]{:S(2)}, u32[]{:S(2)}) collective-permute-start(bf16[2,256,128]{2,1,0:T(8,128)(2,1)S(1)} %pad_maximum_fusion.4), channel_id=1, source_target_pairs={{0,36},{12,48},{24,60},{36,72},{48,84},{60,96},{72,108},{84,120},{... | collective-permute-start | bytes 393224 | tf_op jit(solution)/shard_map/ppermute | solution.py:17
  11.1 13.7 %collective-permute-start.1 = (bf16[2,256,128]{2,1,0:T(8,128)(2,1)S(1)}, bf16[2,256,128]{2,1,0:T(8,128)(2,1)S(1)}, u32[]{:S(2)}, u32[]{:S(2)}) collective-permute-start(bf16[2,256,128]{2,1,0:T(8,128)(2,1)S(1)} %pad_maximum_fusion.4), channel_id=1, source_target_pairs={{0,24},{12,36},{24,48},{36,60},{48,72},{60,84},{72,96},{84,108},{9... | collective-permute-start | bytes 393224 | tf_op jit(solution)/shard_map/ppermute | solution.py:17
  14.5 10.6 %collective-permute-start = (bf16[2,256,128]{2,1,0:T(8,128)(2,1)S(1)}, bf16[2,256,128]{2,1,0:T(8,128)(2,1)S(1)}, u32[]{:S(2)}, u32[]{:S(2)}) collective-permute-start(bf16[2,256,128]{2,1,0:T(8,128)(2,1)S(1)} %pad_maximum_fusion.4), channel_id=1, source_target_pairs={{0,12},{12,24},{24,36},{36,48},{48,60},{60,72},{72,84},{84,96},{96... | collective-permute-start | bytes 393224 | tf_op jit(solution)/shard_map/ppermute | solution.py:17
  18.3 8.8 %collective-permute-start.3 = (bf16[2,256,128]{2,1,0:T(8,128)(2,1)S(1)}, bf16[2,256,128]{2,1,0:T(8,128)(2,1)S(1)}, u32[]{:S(2)}, u32[]{:S(2)}) collective-permute-start(bf16[2,256,128]{2,1,0:T(8,128)(2,1)S(1)} %pad_maximum_fusion.4), channel_id=1, source_target_pairs={{0,48},{12,60},{24,72},{36,84},{48,96},{60,108},{72,120},{84,132},... | collective-permute-start | bytes 393224 | tf_op jit(solution)/shard_map/ppermute | solution.py:17
  27.1 3.9 %copy-start.5 = (bf16[2,256,128]{2,1,0:T(8,128)(2,1)}, bf16[2,256,128]{2,1,0:T(8,128)(2,1)S(1)}, u32[]{:S(2)}) copy-start(bf16[2,256,128]{2,1,0:T(8,128)(2,1)S(1)} %collective-permute-done.3) | copy-start | bytes 393220
  33.9 11.7 %collective-permute-start.4 = (f32[2,256,128]{2,1,0:T(8,128)S(1)}, f32[2,256,128]{2,1,0:T(8,128)S(1)}, u32[]{:S(2)}, u32[]{:S(2)}) collective-permute-start(f32[2,256,128]{2,1,0:T(8,128)S(1)} %pad_maximum_fusion), channel_id=1, source_target_pairs={{12,0},{24,12},{36,24},{48,36},{60,48},{72,60},{84,72},{96,84},{10... | collective-permute-start | bytes 786440 | tf_op jit(solution)/shard_map/ppermute | solution.py:17
  36.5 5.9 %copy-start.6 = (bf16[2,256,128]{2,1,0:T(8,128)(2,1)S(1)}, bf16[2,256,128]{2,1,0:T(8,128)(2,1)}, u32[]{:S(2)}) copy-start(bf16[2,256,128]{2,1,0:T(8,128)(2,1)} %copy-done.5) | copy-start | bytes 393220
  36.5 16.3 %collective-permute-start.5 = (f32[2,256,128]{2,1,0:T(8,128)S(1)}, f32[2,256,128]{2,1,0:T(8,128)S(1)}, u32[]{:S(2)}, u32[]{:S(2)}) collective-permute-start(f32[2,256,128]{2,1,0:T(8,128)S(1)} %pad_maximum_fusion.1), channel_id=1, source_target_pairs={{24,0},{36,12},{48,24},{60,36},{72,48},{84,60},{96,72},{108,84},{1... | collective-permute-start | bytes 786440 | tf_op jit(solution)/shard_map/ppermute | solution.py:17
  39.0 3.7 %copy-start.1 = (bf16[4,256,256]{1,2,0:T(8,128)(2,1)}, bf16[4,256,256]{1,2,0:T(8,128)(2,1)S(1)}, u32[]{:S(2)}) copy-start(bf16[4,256,256]{1,2,0:T(8,128)(2,1)S(1)} %fusion.21) | copy-start | bytes 1572868
  39.4 18.7 %collective-permute-start.6 = (f32[2,256,128]{2,1,0:T(8,128)S(1)}, f32[2,256,128]{2,1,0:T(8,128)S(1)}, u32[]{:S(2)}, u32[]{:S(2)}) collective-permute-start(f32[2,256,128]{2,1,0:T(8,128)S(1)} %pad_maximum_fusion.2), channel_id=1, source_target_pairs={{36,0},{48,12},{60,24},{72,36},{84,48},{96,60},{108,72},{120,84},{... | collective-permute-start | bytes 786440 | tf_op jit(solution)/shard_map/ppermute | solution.py:17
  42.7 2.9 %copy-start.3 = (bf16[4,256,256]{1,2,0:T(8,128)(2,1)}, bf16[4,256,256]{1,2,0:T(8,128)(2,1)S(1)}, u32[]{:S(2)}) copy-start(bf16[4,256,256]{1,2,0:T(8,128)(2,1)S(1)} %fusion.20) | copy-start | bytes 1572868
  43.1 17.5 %collective-permute-start.7 = (f32[2,256,128]{2,1,0:T(8,128)S(1)}, f32[2,256,128]{2,1,0:T(8,128)S(1)}, u32[]{:S(2)}, u32[]{:S(2)}) collective-permute-start(f32[2,256,128]{2,1,0:T(8,128)S(1)} %pad_maximum_fusion.3), channel_id=1, source_target_pairs={{48,0},{60,12},{72,24},{84,36},{96,48},{108,60},{120,72},{132,84},... | collective-permute-start | bytes 786440 | tf_op jit(solution)/shard_map/ppermute | solution.py:17
  62.0 1.2 copy-start.2
  62.0 1.5 copy-start.4
  62.0 1.5 copy-start.7
Sparse Core Ops, SparseCore 0:
  62.1 125.8 all-reduce.1
where the time goes:
time: 199 us
  waiting for transfers between devices  140 us (70%)
  starting transfers between devices  22 us (11%)
  between operations  14.6 us (7%)
  matrix products  12.6 us (6%)
  other arithmetic  5.28 us (3%)
  local copies, waits for them, and re-layouts  4.69 us (2%)
    psum x1, waiting for transfers between devices, on_device(): summed = lax.psum(spread, 'head')  123 us
    ppermute x8, starting transfers between devices, passed_along(): return lax.ppermute(block, axis, route)  22 us
    ppermute x8, waiting for transfers between devices, passed_along(): return lax.ppermute(block, axis, route)  16.7 us
    dot_general x10, matrix products, contract(): jnp.einsum('ipd,jd->pij', first_mat, second_mat, preferred_element_type=j...  4.82 us
  transfers between devices with their start and end apart: 9, of which 5 were waited for; matrix products, arithmetic and copies ran while one was open for 5% of the time, Pallas kernels for 0%

commit v1 on v0

v1 whole, which is shorter than its diff:
```python
import functools

import jax
import jax.numpy as jnp
from jax import lax
from jax.experimental import pallas as pl
from jax.experimental.pallas import tpu as pltpu
from jax.sharding import PartitionSpec as P

GROUP = 8
BLOCK = 128
REACH = 8
MASKED = -1e30
LOG2E = 1.4426950408889634
MESH = pl.DeviceIdType.MESH
CHUNKS = 4

NT = (((1,), (1,)), ((), ()))
NN = (((1,), (0,)), ((), ()))
TN = (((0,), (0,)), ((), ()))


def dot(a, b, dims):
    return lax.dot_general(a, b, dims, preferred_element_type=jnp.float32)


def kernel(
    n_ctx, n_head, heads, docs,
    docs_ref, q_hbm, do_hbm, k_hbm, v_hbm,
    dq_out, kv_out,
    q_ref, do_ref, kw, vw, e_ref, dp_ref, stat, ds_ref, own, sb, rb, og, dq_ref,
    load_sem, a_send, a_recv, b_send, b_recv, c_send, c_recv, out_sem,
):
    width = q_ref.shape[1]
    shard = 2 * BLOCK
    rows = BLOCK * heads
    scale = width ** -0.5
    to_log2 = scale * LOG2E
    s = lax.axis_index("ctx")
    h = lax.axis_index("head")
    role = lax.rem(h, 2)
    partner = h + 1 - 2 * role
    other = lax.rem(h - 1 + 2 * role + n_head, n_head)
    up = lax.rem(h + 1, n_head)
    down = lax.rem(h + n_head - 1, n_head)
    group = h * heads // GROUP

    def ctx(delta):
        return lax.rem(s + delta + n_ctx, n_ctx)

    loads = [
        pltpu.make_async_copy(k_hbm.at[group], kw.at[pl.ds(7 * BLOCK, shard)], load_sem.at[0]),
        pltpu.make_async_copy(v_hbm.at[group], vw.at[pl.ds(7 * BLOCK, shard)], load_sem.at[1]),
        pltpu.make_async_copy(q_hbm, q_ref, load_sem.at[2]),
        pltpu.make_async_copy(do_hbm, do_ref, load_sem.at[3]),
    ]
    for copy in loads:
        copy.start()

    barrier = pltpu.get_barrier_semaphore()
    peers = [(ctx(d), h) for d in range(-4, 5) if d != 0]
    peers += [(ctx(d), partner) for d in range(-4, 5)] + [(s, other)]
    for peer in peers:
        pl.semaphore_signal(barrier, inc=1, device_id=peer, device_id_type=MESH)
    pl.semaphore_wait(barrier, len(peers))

    sends = []
    fetch = {}
    for d in (4, 3, 2, 1):
        size, first = (shard, 0) if d < 4 else (BLOCK, BLOCK)
        at = (7 - 2 * d) * BLOCK + first
        for i, (src, dst) in enumerate(((k_hbm, kw), (v_hbm, vw))):
            copy = pltpu.make_async_remote_copy(
                src_ref=src.at[group, pl.ds(first, size)],
                dst_ref=dst.at[pl.ds(at, size)],
                send_sem=a_send.at[d - 1, i],
                recv_sem=a_recv.at[d - 1, i],
                device_id=(ctx(d), h),
                device_id_type=MESH,
            )
            copy.start()
            sends.append(copy)
            fetch[d, i] = copy

    before = []
    for qb in range(2):
        at = 2 * s + qb
        total = jnp.int32(0)
        start = jnp.int32(0)
        for i in range(docs):
            start = jnp.where(total <= at, total, start)
            total = total + docs_ref[i]
        before.append(at - start)

    for copy in loads:
        copy.wait()

    key_at = lax.broadcasted_iota(jnp.int32, (BLOCK, rows), 0)
    query_at = lax.broadcasted_iota(jnp.int32, (BLOCK, rows), 1) // heads
    causal = key_at <= query_at

    def pair(qb, w):
        back = 7 + qb - w
        q = q_ref[pl.ds(qb * rows, rows), :]
        do = do_ref[pl.ds(qb * rows, rows), :]
        scores = dot(kw[pl.ds(w * BLOCK, BLOCK), :], q, NT)
        if back == 0:
            scores = jnp.where(causal, scores, MASKED)
        top = jnp.max(scores, axis=0, keepdims=True) * to_log2
        e = jnp.exp2(scores * to_log2 - top)
        dp = dot(vw[pl.ds(w * BLOCK, BLOCK), :], do, NT)
        at = w - qb
        e_ref[qb, pl.ds(at * BLOCK, BLOCK), :] = e
        dp_ref[qb, pl.ds(at * BLOCK, BLOCK), :] = dp
        bias = jnp.where(back <= before[qb], jnp.float32(0), jnp.float32(MASKED))
        stat[qb, 0, pl.ds(at, 1), :] = top + bias
        stat[qb, 1, pl.ds(at, 1), :] = jnp.sum(e, axis=0, keepdims=True)
        stat[qb, 2, pl.ds(at, 1), :] = jnp.sum(e * dp, axis=0, keepdims=True)

    pair(0, 7)
    pair(1, 7)
    pair(1, 8)
    for d in (1, 2, 3, 4):
        fetch[d, 0].wait_recv()
        fetch[d, 1].wait_recv()
        if d < 4:
            for w in (7 - 2 * d, 8 - 2 * d):
                pair(0, w)
                pair(1, w)
        else:
            pair(0, 0)

    factors, dots = [], []
    for qb in range(2):
        tops = stat[qb, 0]
        part = jnp.exp2(tops - jnp.max(tops, axis=0, keepdims=True))
        inv = 1.0 / jnp.sum(stat[qb, 1] * part, axis=0, keepdims=True)
        factors.append(part * inv)
        dots.append(jnp.sum(stat[qb, 2] * part, axis=0, keepdims=True) * inv)

    back_sends = []
    back_recv = {}

    def key_block(w):
        grads = [None, None]
        for qb in range(2):
            at = w - qb
            if not 0 <= at < REACH:
                continue
            probs = e_ref[qb, pl.ds(at * BLOCK, BLOCK), :] * factors[qb][at : at + 1]
            dscore = (probs * (dp_ref[qb, pl.ds(at * BLOCK, BLOCK), :] - dots[qb])).astype(jnp.bfloat16)
            ds_ref[qb, pl.ds(at * BLOCK, BLOCK), :] = dscore
            terms = (
                dot(dscore, q_ref[pl.ds(qb * rows, rows), :], NN),
                dot(probs.astype(jnp.bfloat16), do_ref[pl.ds(qb * rows, rows), :], NN),
            )
            grads = [t if g is None else g + t for g, t in zip(grads, terms)]
        grads[0] = grads[0] * scale
        d, half = (8 - w) // 2, (w + 1) % 2
        for i in range(2):
            sb[w, i] = grads[i].astype(jnp.bfloat16)
            if d == 0:
                own[i, pl.ds(half * BLOCK, BLOCK), :] = grads[i]
        for plane, row in enumerate((h, partner)):
            if d == 0 and plane == 0:
                continue
            which = role if plane == 0 else 1 - role
            copy = pltpu.make_async_remote_copy(
                src_ref=sb.at[w, which],
                dst_ref=rb.at[plane, d, pl.ds(half * BLOCK, BLOCK)],
                send_sem=b_send.at[plane, d, half],
                recv_sem=b_recv.at[plane, d, half],
                device_id=(ctx(-d), row),
                device_id_type=MESH,
            )
            copy.start()
            back_sends.append(copy)
            back_recv[plane, d, half] = copy

    for w in (1, 3, 5, 7, 0, 2, 4, 6, 8):
        key_block(w)

    for qb in range(2):
        grad = dot(kw[pl.ds(qb * BLOCK, REACH * BLOCK), :], ds_ref[qb], TN)
        dq_ref[pl.ds(qb * rows, rows), :] = (jnp.transpose(grad) * scale).astype(jnp.bfloat16)
    dq_copy = pltpu.make_async_copy(dq_ref, dq_out, out_sem.at[n_head])
    dq_copy.start()

    piece = shard // CHUNKS
    far = n_head // 2

    def hop(step, chunk, way):
        origin = lax.rem(h + n_head - step, n_head) if way == 0 else lax.rem(h + step, n_head)
        part = og.at[origin, pl.ds(chunk * piece, piece)]
        return pltpu.make_async_remote_copy(
            src_ref=part,
            dst_ref=part,
            send_sem=c_send.at[way, step, chunk],
            recv_sem=c_recv.at[way, step, chunk],
            device_id=(s, up if way == 0 else down),
            device_id_type=MESH,
        )

    def hops(chunk, way):
        return far if (chunk % 2 == 0) == (way == 0) else n_head - 1 - far

    ring = {}
    for half in range(2):
        total = own[role, pl.ds(half * BLOCK, BLOCK), :]
        for (plane, d, at), copy in back_recv.items():
            if at == half:
                copy.wait_recv()
                total = total + rb[plane, d, pl.ds(half * BLOCK, BLOCK), :].astype(jnp.float32)
        og[h, pl.ds(half * BLOCK, BLOCK), :] = total.astype(jnp.bfloat16)
        for chunk in range(half * CHUNKS // 2, (half + 1) * CHUNKS // 2):
            for way in range(2):
                ring[0, chunk, way] = hop(0, chunk, way)
                ring[0, chunk, way].start()

    outs = []

    def put(origin, index):
        copy = pltpu.make_async_copy(og.at[origin], kv_out.at[lax.rem(origin, 2), origin // 2], out_sem.at[index])
        copy.start()
        outs.append(copy)

    put(h, 0)
    for step in range(1, far + 1):
        for chunk in range(CHUNKS):
            for way in range(2):
                if step <= hops(chunk, way):
                    ring[step - 1, chunk, way].wait_recv()
                if step < hops(chunk, way):
                    ring[step, chunk, way] = hop(step, chunk, way)
                    ring[step, chunk, way].start()
        put(lax.rem(h + n_head - step, n_head), 2 * step - 1)
        if step < far:
            put(lax.rem(h + step, n_head), 2 * step)

    for copy in sends + back_sends + list(ring.values()):
        copy.wait_send()
    dq_copy.wait()
    for copy in outs:
        copy.wait()


def on_device(query_heads, key_head, value_head, out_grad, doc_blocks, n_ctx, n_head):
    tokens, heads, width = query_heads.shape
    kv_count = key_head.shape[1]
    rows = BLOCK * heads
    flat = lambda x: x.reshape(tokens * heads, width)
    dma = pltpu.SemaphoreType.DMA
    bf16, f32 = jnp.bfloat16, jnp.float32
    window = (REACH + 1) * BLOCK
    dq, kv = pl.pallas_call(
        functools.partial(kernel, n_ctx, n_head, heads, doc_blocks.shape[0]),
        out_shape=(
            jax.ShapeDtypeStruct((tokens * heads, width), bf16),
            jax.ShapeDtypeStruct((2, kv_count, tokens, width), bf16),
        ),
        in_specs=[pl.BlockSpec(memory_space=pltpu.SMEM)] + [pl.BlockSpec(memory_space=pl.ANY)] * 4,
        out_specs=(pl.BlockSpec(memory_space=pl.ANY),) * 2,
        scratch_shapes=[
            pltpu.VMEM((tokens * heads, width), bf16),
            pltpu.VMEM((tokens * heads, width), bf16),
            pltpu.VMEM((window, width), bf16),
            pltpu.VMEM((window, width), bf16),
            pltpu.VMEM((2, REACH * BLOCK, rows), f32),
            pltpu.VMEM((2, REACH * BLOCK, rows), f32),
            pltpu.VMEM((2, 3, REACH, rows), f32),
            pltpu.VMEM((2, REACH * BLOCK, rows), bf16),
            pltpu.VMEM((2, 2 * BLOCK, width), f32),
            pltpu.VMEM((REACH + 1, 2, BLOCK, width), bf16),
            pltpu.VMEM((2, 5, 2 * BLOCK, width), bf16),
            pltpu.VMEM((n_head, tokens, width), bf16),
            pltpu.VMEM((tokens * heads, width), bf16),
            dma((4,)),
            dma((4, 2)),
            dma((4, 2)),
            dma((2, 5, 2)),
            dma((2, 5, 2)),
            dma((2, n_head // 2, CHUNKS)),
            dma((2, n_head // 2, CHUNKS)),
            dma((n_head + 1,)),
        ],
        compiler_params=pltpu.CompilerParams(
            collective_id=0, has_side_effects=True, vmem_limit_bytes=48 * 1024 * 1024
        ),
        name="attention_backward",
    )(
        doc_blocks,
        flat(query_heads),
        flat(out_grad),
        jnp.transpose(key_head, (1, 0, 2)),
        jnp.transpose(value_head, (1, 0, 2)),
    )
    kv = jnp.transpose(kv, (0, 2, 1, 3))
    return dq.reshape(tokens, heads, width), kv[0], kv[1]


def solution(mesh):
    return jax.shard_map(
        functools.partial(on_device, n_ctx=mesh.shape["ctx"], n_head=mesh.shape["head"]),
        mesh=mesh,
        in_specs=(
            P("ctx", "head", None),
            P("ctx", None, None),
            P("ctx", None, None),
            P("ctx", "head", None),
            P(),
        ),
        out_specs=(P("ctx", "head", None), P("ctx", None, None), P("ctx", None, None)),
        check_vma=False,
    )
```

time: 199 us -> 67.7 us (0.34)
  the two profiles are of different devices: /device:TPU:6 before, /device:TPU:30 now
where the time goes in v1:
time: 67.7 us; the launch traced here: 67.4 us
  Pallas kernels  60.6 us (90%)
  local copies, waits for them, and re-layouts  6.17 us (9%)
    pallas_call x1, Pallas kernels, on_device(): pl.pallas_call(functools.partial(kernel, n_ctx, n_head, heads, doc_blocks...  60.6 us
    unnamed x11, local copies, waits for them, and re-layouts  5.24 us

profile of v1, /device:TPU:30, one launch (start us, length us, event | category | flops | bytes accessed | tf_op | source)
XLA Modules:
  0.0 67.4 jit_solution(14959423557357324541)
XLA Ops:
  0.6 0.0 copy-start.4
  0.6 0.6 copy-done.4
  1.3 0.0 copy-start
  1.3 1.0 %copy-done = bf16[256,6,128]{2,0,1:T(8,128)(2,1)S(1)} copy-done((bf16[256,6,128]{2,0,1:T(8,128)(2,1)S(1)}, bf16[256,6,128]{2,0,1:T(8,128)(2,1)}, u32[]{:S(2)}) %copy-start) | copy-done | bytes 393240
  2.3 0.0 copy-start.1
  2.3 1.0 %copy-done.1 = bf16[256,6,128]{2,0,1:T(8,128)(2,1)S(1)} copy-done((bf16[256,6,128]{2,0,1:T(8,128)(2,1)S(1)}, bf16[256,6,128]{2,0,1:T(8,128)(2,1)}, u32[]{:S(2)}) %copy-start.1) | copy-done | bytes 393240
  3.3 0.0 copy-start.2
  3.3 0.9 %copy-done.2 = bf16[256,4,128]{2,1,0:T(4,128)(2,1)S(1)} copy-done((bf16[256,4,128]{2,1,0:T(4,128)(2,1)S(1)}, bf16[256,4,128]{2,1,0:T(4,128)(2,1)}, u32[]{:S(2)}) %copy-start.2) | copy-done | bytes 262168
  4.2 0.0 copy-start.3
  4.2 0.9 %copy-done.3 = bf16[256,4,128]{2,1,0:T(4,128)(2,1)S(1)} copy-done((bf16[256,4,128]{2,1,0:T(4,128)(2,1)S(1)}, bf16[256,4,128]{2,1,0:T(4,128)(2,1)}, u32[]{:S(2)}) %copy-start.3) | copy-done | bytes 262168
  5.2 60.6 %attention_backward.1 = (bf16[1024,128]{1,0:T(8,128)(2,1)S(1)}, bf16[2,6,256,128]{3,2,1,0:T(8,128)(2,1)S(1)}) custom-call(s32[32]{0:T(128)S(1)} %copy-done.4, bf16[1024,128]{1,0:T(8,128)(2,1)S(1)} %bitcast.13, bf16[1024,128]{1,0:T(8,128)(2,1)S(1)} %bitcast.14, bf16[6,256,128]{2,1,0:T(8,128)(2,1)S(1)} %bitcast.11, bf16[6,256,128]{2,1,0:T(8,128)(2,1)S(1)} %bitcast.12), custom_call_target="tpu_custom_call" | custom-call | tf_op jit(solution)/shard_map/attention_backward/pallas_call | solution.py:255
  65.8 0.9 %slice_bitcast_fusion = (bf16[256,6,128]{2,0,1:T(8,128)(2,1)}, bf16[256,6,128]{2,0,1:T(8,128)(2,1)}) fusion(bf16[2,256,6,128]{3,1,2,0:T(8,128)(2,1)S(1)} %bitcast.10), kind=kLoop, calls=%fused_computation | loop fusion | bytes 1572864 | tf_op jit(solution)/shard_map/squeeze | solution.py:298
  66.7 0.7 %copy.9 = bf16[256,4,128]{2,1,0:T(4,128)(2,1)} copy(bf16[256,4,128]{2,1,0:T(4,128)(2,1)S(1)} %bitcast.15) | data formatting | bytes 524288
Async XLA Ops:
  0.6 0.7 copy-start.4
  1.3 1.0 %copy-start = (bf16[256,6,128]{2,0,1:T(8,128)(2,1)S(1)}, bf16[256,6,128]{2,0,1:T(8,128)(2,1)}, u32[]{:S(2)}) copy-start(bf16[256,6,128]{2,0,1:T(8,128)(2,1)} %param.6) | copy-start | bytes 1179652
  2.3 1.0 %copy-start.1 = (bf16[256,6,128]{2,0,1:T(8,128)(2,1)S(1)}, bf16[256,6,128]{2,0,1:T(8,128)(2,1)}, u32[]{:S(2)}) copy-start(bf16[256,6,128]{2,0,1:T(8,128)(2,1)} %param.7) | copy-start | bytes 1179652
  3.3 0.9 %copy-start.2 = (bf16[256,4,128]{2,1,0:T(4,128)(2,1)S(1)}, bf16[256,4,128]{2,1,0:T(4,128)(2,1)}, u32[]{:S(2)}) copy-start(bf16[256,4,128]{2,1,0:T(4,128)(2,1)} %param.5) | copy-start | bytes 786436
  4.2 0.9 %copy-start.3 = (bf16[256,4,128]{2,1,0:T(4,128)(2,1)S(1)}, bf16[256,4,128]{2,1,0:T(4,128)(2,1)}, u32[]{:S(2)}) copy-start(bf16[256,4,128]{2,1,0:T(4,128)(2,1)} %param.8) | copy-start | bytes 786436

commit v2 on v1

--- a/solution.py
+++ b/solution.py
@@ -45,12 +45,18 @@
     down = lax.rem(h + n_head - 1, n_head)
     group = h * heads // GROUP
 
+    core = lax.rem(s, 2)
+    sibling = s + 1 - 2 * core
+
     def ctx(delta):
         return lax.rem(s + delta + n_ctx, n_ctx)
 
+    def slot(d, first=0, size=shard):
+        return pl.ds((8 - 2 * d) * BLOCK + first, size)
+
     loads = [
-        pltpu.make_async_copy(k_hbm.at[group], kw.at[pl.ds(7 * BLOCK, shard)], load_sem.at[0]),
-        pltpu.make_async_copy(v_hbm.at[group], vw.at[pl.ds(7 * BLOCK, shard)], load_sem.at[1]),
+        pltpu.make_async_copy(k_hbm.at[group], kw.at[slot(0)], load_sem.at[0]),
+        pltpu.make_async_copy(v_hbm.at[group], vw.at[slot(0)], load_sem.at[1]),
         pltpu.make_async_copy(q_hbm, q_ref, load_sem.at[2]),
         pltpu.make_async_copy(do_hbm, do_ref, load_sem.at[3]),
     ]
@@ -64,23 +70,55 @@
         pl.semaphore_signal(barrier, inc=1, device_id=peer, device_id_type=MESH)
     pl.semaphore_wait(barrier, len(peers))
 
-    sends = []
-    fetch = {}
-    for d in (4, 3, 2, 1):
-        size, first = (shard, 0) if d < 4 else (BLOCK, BLOCK)
-        at = (7 - 2 * d) * BLOCK + first
-        for i, (src, dst) in enumerate(((k_hbm, kw), (v_hbm, vw))):
-            copy = pltpu.make_async_remote_copy(
-                src_ref=src.at[group, pl.ds(first, size)],
-                dst_ref=dst.at[pl.ds(at, size)],
-                send_sem=a_send.at[d - 1, i],
-                recv_sem=a_recv.at[d - 1, i],
-                device_id=(ctx(d), h),
-                device_id_type=MESH,
-            )
-            copy.start()
-            sends.append(copy)
-            fetch[d, i] = copy
+    pairs = ((k_hbm, kw), (v_hbm, vw))
+
+    def push(i, src, dst, sem, target):
+        return pltpu.make_async_remote_copy(
+            src_ref=src,
+            dst_ref=dst,
+            send_sem=a_send.at[sem, i],
+            recv_sem=a_recv.at[sem, i],
+            device_id=(target, h),
+            device_id_type=MESH,
+        )
+
+    def far_half(i, half):
+        src, dst = pairs[i]
+        at = half * BLOCK
+        return push(i, src.at[group, pl.ds(at, BLOCK)], dst.at[slot(4, at, BLOCK)], half, ctx(4))
+
+    def near(i):
+        src, dst = pairs[i]
+        return push(i, src.at[group], dst.at[slot(2)], 2, ctx(2))
+
+    def across_near(i):
+        dst = pairs[i][1]
+        to = pl.ds((2 + 4 * core) * BLOCK, shard)
+        return push(i, dst.at[slot(2)], dst.at[to], 3, sibling)
+
+    def across_own(i):
+        src, dst = pairs[i]
+        return push(i, src.at[group], dst.at[slot(1)], 4, sibling)
+
+    def across_far(i):
+        dst = pairs[i][1]
+        return push(i, dst.at[slot(4)], dst.at[slot(3)], 4, sibling)
+
+    for i in range(2):
+        far_half(i, 1).start()
+
+    @pl.when(core == 1)
+    def _():
+        for i in range(2):
+            far_half(i, 0).start()
+
+    for i in range(2):
+        near(i).start()
+
+    @pl.when(core == 0)
+    def _():
+        for i in range(2):
+            across_own(i).start()
 
     before = []
     for qb in range(2):
@@ -103,12 +141,12 @@
         back = 7 + qb - w
         q = q_ref[pl.ds(qb * rows, rows), :]
         do = do_ref[pl.ds(qb * rows, rows), :]
-        scores = dot(kw[pl.ds(w * BLOCK, BLOCK), :], q, NT)
+        scores = dot(kw[pl.ds((w + 1) * BLOCK, BLOCK), :], q, NT)
         if back == 0:
             scores = jnp.where(causal, scores, MASKED)
         top = jnp.max(scores, axis=0, keepdims=True) * to_log2
         e = jnp.exp2(scores * to_log2 - top)
-        dp = dot(vw[pl.ds(w * BLOCK, BLOCK), :], do, NT)
+        dp = dot(vw[pl.ds((w + 1) * BLOCK, BLOCK), :], do, NT)
         at = w - qb
         e_ref[qb, pl.ds(at * BLOCK, BLOCK), :] = e
         dp_ref[qb, pl.ds(at * BLOCK, BLOCK), :] = dp
@@ -120,15 +158,28 @@
     pair(0, 7)
     pair(1, 7)
     pair(1, 8)
-    for d in (1, 2, 3, 4):
-        fetch[d, 0].wait_recv()
-        fetch[d, 1].wait_recv()
-        if d < 4:
-            for w in (7 - 2 * d, 8 - 2 * d):
-                pair(0, w)
-                pair(1, w)
-        else:
-            pair(0, 0)
+    for i in range(2):
+        far_half(i, 1).wait_recv()
+
+    @pl.when(core == 1)
+    def _():
+        for i in range(2):
+            far_half(i, 0).wait_recv()
+            across_far(i).start()
+
+    for i in range(2):
+        near(i).wait_recv()
+        across_near(i).start()
+    pair(0, 0)
+    for w in (3, 4):
+        pair(0, w)
+        pair(1, w)
+    for i in range(2):
+        across_far(i).wait_recv()
+        across_near(i).wait_recv()
+    for w in (1, 2, 5, 6):
+        pair(0, w)
+        pair(1, w)
 
     factors, dots = [], []
     for qb in range(2):
@@ -181,7 +232,7 @@
         key_block(w)
 
     for qb in range(2):
-        grad = dot(kw[pl.ds(qb * BLOCK, REACH * BLOCK), :], ds_ref[qb], TN)
+        grad = dot(kw[pl.ds((qb + 1) * BLOCK, REACH * BLOCK), :], ds_ref[qb], TN)
         dq_ref[pl.ds(qb * rows, rows), :] = (jnp.transpose(grad) * scale).astype(jnp.bfloat16)
     dq_copy = pltpu.make_async_copy(dq_ref, dq_out, out_sem.at[n_head])
     dq_copy.start()
@@ -204,7 +255,6 @@
     def hops(chunk, way):
         return far if (chunk % 2 == 0) == (way == 0) else n_head - 1 - far
 
-    ring = {}
     for half in range(2):
         total = own[role, pl.ds(half * BLOCK, BLOCK), :]
         for (plane, d, at), copy in back_recv.items():
@@ -214,8 +264,7 @@
         og[h, pl.ds(half * BLOCK, BLOCK), :] = total.astype(jnp.bfloat16)
         for chunk in range(half * CHUNKS // 2, (half + 1) * CHUNKS // 2):
             for way in range(2):
-                ring[0, chunk, way] = hop(0, chunk, way)
-                ring[0, chunk, way].start()
+                hop(0, chunk, way).start()
 
     outs = []
 
@@ -225,20 +274,42 @@
         outs.append(copy)
 
     put(h, 0)
+
+    def advance(step, way):
+        for chunk in range(CHUNKS):
+            if step <= hops(chunk, way):
+                hop(step - 1, chunk, way).wait_recv()
+            if step < hops(chunk, way):
+                hop(step, chunk, way).start()
+
     for step in range(1, far + 1):
-        for chunk in range(CHUNKS):
-            for way in range(2):
-                if step <= hops(chunk, way):
-                    ring[step - 1, chunk, way].wait_recv()
-                if step < hops(chunk, way):
-                    ring[step, chunk, way] = hop(step, chunk, way)
-                    ring[step, chunk, way].start()
-        put(lax.rem(h + n_head - step, n_head), 2 * step - 1)
+        pl.when(step <= h)(functools.partial(advance, step, 0))
+    for step in range(1, far + 1):
+        advance(step, 1)
         if step < far:
             put(lax.rem(h + step, n_head), 2 * step)
-
-    for copy in sends + back_sends + list(ring.values()):
+    for step in range(1, far + 1):
+        pl.when(step > h)(functools.partial(advance, step, 0))
+    for step in range(1, far + 1):
+        put(lax.rem(h + n_head - step, n_head), 2 * step - 1)
+
+    for copy in back_sends:
         copy.wait_send()
+    for i in range(2):
+        far_half(i, 1).wait_send()
+        near(i).wait_send()
+        across_near(i).wait_send()
+        across_own(i).wait_send()
+
+    @pl.when(core == 1)
+    def _():
+        for i in range(2):
+            far_half(i, 0).wait_send()
+
+    for way in range(2):
+        for chunk in range(CHUNKS):
+            for step in range(hops(chunk, way)):
+                hop(step, chunk, way).wait_send()
     dq_copy.wait()
     for copy in outs:
         copy.wait()
@@ -251,7 +322,7 @@
     flat = lambda x: x.reshape(tokens * heads, width)
     dma = pltpu.SemaphoreType.DMA
     bf16, f32 = jnp.bfloat16, jnp.float32
-    window = (REACH + 1) * BLOCK
+    window = (REACH + 2) * BLOCK
     dq, kv = pl.pallas_call(
         functools.partial(kernel, n_ctx, n_head, heads, doc_blocks.shape[0]),
         out_shape=(
@@ -275,8 +346,8 @@
             pltpu.VMEM((n_head, tokens, width), bf16),
             pltpu.VMEM((tokens * heads, width), bf16),
             dma((4,)),
-            dma((4, 2)),
-            dma((4, 2)),
+            dma((5, 2)),
+            dma((5, 2)),
             dma((2, 5, 2)),
             dma((2, 5, 2)),
             dma((2, n_head // 2, CHUNKS)),
@@ -284,7 +355,7 @@
             dma((n_head + 1,)),
         ],
         compiler_params=pltpu.CompilerParams(
-            collective_id=0, has_side_effects=True, vmem_limit_bytes=48 * 1024 * 1024
+            collective_id=0, has_side_effects=True, vmem_limit_bytes=67043328
         ),
         name="attention_backward",
     )(

time: 67.7 us -> 78.2 us (1.16)
  the two profiles are of different devices: /device:TPU:30 before, /device:TPU:382 now
where the time goes in v2:
time: 78.2 us; the launch traced here: 78 us
  Pallas kernels  74.6 us (95%)
  local copies, waits for them, and re-layouts  2.79 us (4%)
    pallas_call x1, Pallas kernels, on_device(): pl.pallas_call(functools.partial(kernel, n_ctx, n_head, heads, doc_blocks...  74.6 us
    squeeze x1, local copies, waits for them, and re-layouts, on_device(): return (dq.reshape(tokens, heads, width), kv[0], kv[1])  2.08 us

profile of v2, /device:TPU:382, one launch (start us, length us, event | category | flops | bytes accessed | tf_op | source)
XLA Modules:
  0.0 78.0 jit_solution(16875311872115315456)
XLA Ops:
  0.6 74.6 %attention_backward.1 = (bf16[1024,128]{1,0:T(8,128)(2,1)}, bf16[2,6,256,128]{3,2,1,0:T(8,128)(2,1)}) custom-call(s32[32]{0:T(128)} %docs_ref.1, bf16[1024,128]{1,0:T(8,128)(2,1)} %bitcast.13, bf16[1024,128]{1,0:T(8,128)(2,1)} %bitcast.14, bf16[6,256,128]{2,1,0:T(8,128)(2,1)} %bitcast.11, bf16[6,256,128]{2,1,0:T(8,128)(2,1)} %bitcast.12), custom_call_target="tpu_custom_call" | custom-call | tf_op jit(solution)/shard_map/attention_backward/pallas_call | solution.py:326
  75.2 0.0 copy-start
  75.3 2.1 %slice_bitcast_fusion = (bf16[256,6,128]{2,0,1:T(8,128)(2,1)}, bf16[256,6,128]{2,0,1:T(8,128)(2,1)}) fusion(bf16[2,256,6,128]{3,1,2,0:T(8,128)(2,1)} %bitcast.10), kind=kLoop, calls=%fused_computation | loop fusion | bytes 1572864 | tf_op jit(solution)/shard_map/squeeze | solution.py:369
  77.3 0.0 copy-done
  77.3 0.7 copy.9
Async XLA Ops:
  75.2 2.1 %copy-start = (bf16[1024,128]{1,0:T(8,128)(2,1)S(1)}, bf16[1024,128]{1,0:T(8,128)(2,1)}, u32[]{:S(2)}) copy-start(bf16[1024,128]{1,0:T(8,128)(2,1)} %get-tuple-element.5) | copy-start | bytes 786436

commit v3 on v2

--- a/solution.py
+++ b/solution.py
@@ -26,9 +26,9 @@
 
 def kernel(
     n_ctx, n_head, heads, docs,
-    docs_ref, q_hbm, do_hbm, k_hbm, v_hbm,
+    docs_hbm, q_hbm, do_hbm, k_hbm, v_hbm,
     dq_out, kv_out,
-    q_ref, do_ref, kw, vw, e_ref, dp_ref, stat, ds_ref, own, sb, rb, og, dq_ref,
+    docs_ref, q_ref, do_ref, kw, vw, e_ref, dp_ref, stat, ds_ref, own, sb, rb, og, dq_ref,
     load_sem, a_send, a_recv, b_send, b_recv, c_send, c_recv, out_sem,
 ):
     width = q_ref.shape[1]
@@ -41,8 +41,6 @@
     role = lax.rem(h, 2)
     partner = h + 1 - 2 * role
     other = lax.rem(h - 1 + 2 * role + n_head, n_head)
-    up = lax.rem(h + 1, n_head)
-    down = lax.rem(h + n_head - 1, n_head)
     group = h * heads // GROUP
 
     core = lax.rem(s, 2)
@@ -59,13 +57,14 @@
         pltpu.make_async_copy(v_hbm.at[group], vw.at[slot(0)], load_sem.at[1]),
         pltpu.make_async_copy(q_hbm, q_ref, load_sem.at[2]),
         pltpu.make_async_copy(do_hbm, do_ref, load_sem.at[3]),
+        pltpu.make_async_copy(docs_hbm, docs_ref, load_sem.at[4]),
     ]
     for copy in loads:
         copy.start()
 
     barrier = pltpu.get_barrier_semaphore()
     peers = [(ctx(d), h) for d in range(-4, 5) if d != 0]
-    peers += [(ctx(d), partner) for d in range(-4, 5)] + [(s, other)]
+    peers += [(ctx(d), partner) for d in range(-4, 5)] + [(s, other), (s, lax.rem(h + 2, n_head)), (s, lax.rem(h + n_head - 2, n_head))]
     for peer in peers:
         pl.semaphore_signal(barrier, inc=1, device_id=peer, device_id_type=MESH)
     pl.semaphore_wait(barrier, len(peers))
@@ -120,6 +119,9 @@
         for i in range(2):
             across_own(i).start()
 
+    for copy in loads:
+        copy.wait()
+
     before = []
     for qb in range(2):
         at = 2 * s + qb
@@ -129,9 +131,6 @@
             start = jnp.where(total <= at, total, start)
             total = total + docs_ref[i]
         before.append(at - start)
-
-    for copy in loads:
-        copy.wait()
 
     key_at = lax.broadcasted_iota(jnp.int32, (BLOCK, rows), 0)
     query_at = lax.broadcasted_iota(jnp.int32, (BLOCK, rows), 1) // heads
@@ -240,20 +239,28 @@
     piece = shard // CHUNKS
     far = n_head // 2
 
-    def hop(step, chunk, way):
-        origin = lax.rem(h + n_head - step, n_head) if way == 0 else lax.rem(h + step, n_head)
-        part = og.at[origin, pl.ds(chunk * piece, piece)]
+    def row(distance, way):
+        return lax.rem(h + n_head + distance * (1 - 2 * way), n_head)
+
+    def hop(way, step, chunk):
+        relay = (step - 1) // 2 * 2
+        part = og.at[row(-relay, way), pl.ds(chunk * piece, piece)]
         return pltpu.make_async_remote_copy(
             src_ref=part,
             dst_ref=part,
-            send_sem=c_send.at[way, step, chunk],
-            recv_sem=c_recv.at[way, step, chunk],
-            device_id=(s, up if way == 0 else down),
+            send_sem=c_send.at[way, step - 1, chunk],
+            recv_sem=c_recv.at[way, step - 1, chunk],
+            device_id=(s, row(step - relay, way)),
             device_id_type=MESH,
         )
 
-    def hops(chunk, way):
-        return far if (chunk % 2 == 0) == (way == 0) else n_head - 1 - far
+    def steps(way, chunk):
+        return far if chunk % 2 == way else n_head - 1 - far
+
+    def pass_on(relay, way, chunk):
+        for step in (relay + 2, relay + 1):
+            if step <= steps(way, chunk):
+                hop(way, step, chunk).start()
 
     for half in range(2):
         total = own[role, pl.ds(half * BLOCK, BLOCK), :]
@@ -264,34 +271,35 @@
         og[h, pl.ds(half * BLOCK, BLOCK), :] = total.astype(jnp.bfloat16)
         for chunk in range(half * CHUNKS // 2, (half + 1) * CHUNKS // 2):
             for way in range(2):
-                hop(0, chunk, way).start()
+                pass_on(0, way, chunk)
 
     outs = []
 
-    def put(origin, index):
-        copy = pltpu.make_async_copy(og.at[origin], kv_out.at[lax.rem(origin, 2), origin // 2], out_sem.at[index])
+    def put(of, index):
+        copy = pltpu.make_async_copy(og.at[of], kv_out.at[lax.rem(of, 2), of // 2], out_sem.at[index])
         copy.start()
         outs.append(copy)
 
+    def arrive(step, way, chunk):
+        if step <= steps(way, chunk):
+            hop(way, step, chunk).wait_recv()
+
     put(h, 0)
-
-    def advance(step, way):
+    for step in (2, 4):
         for chunk in range(CHUNKS):
-            if step <= hops(chunk, way):
-                hop(step - 1, chunk, way).wait_recv()
-            if step < hops(chunk, way):
-                hop(step, chunk, way).start()
-
-    for step in range(1, far + 1):
-        pl.when(step <= h)(functools.partial(advance, step, 0))
-    for step in range(1, far + 1):
-        advance(step, 1)
-        if step < far:
-            put(lax.rem(h + step, n_head), 2 * step)
-    for step in range(1, far + 1):
-        pl.when(step > h)(functools.partial(advance, step, 0))
-    for step in range(1, far + 1):
-        put(lax.rem(h + n_head - step, n_head), 2 * step - 1)
+            for way in range(2):
+                arrive(step, way, chunk)
+                pass_on(step, way, chunk)
+    for step in (2, 4, 1, 3, 5):
+        for way in range(2):
+            if step % 2:
+                for chunk in range(CHUNKS):
+                    arrive(step, way, chunk)
+            put(row(-step, way), 2 * step - 1 + way)
+    for chunk in range(CHUNKS):
+        for way in range(2):
+            arrive(far, way, chunk)
+    put(row(far, 0), 2 * far - 1)
 
     for copy in back_sends:
         copy.wait_send()
@@ -308,8 +316,8 @@
 
     for way in range(2):
         for chunk in range(CHUNKS):
-            for step in range(hops(chunk, way)):
-                hop(step, chunk, way).wait_send()
+            for step in range(1, steps(way, chunk) + 1):
+                hop(way, step, chunk).wait_send()
     dq_copy.wait()
     for copy in outs:
         copy.wait()
@@ -329,9 +337,10 @@
             jax.ShapeDtypeStruct((tokens * heads, width), bf16),
             jax.ShapeDtypeStruct((2, kv_count, tokens, width), bf16),
         ),
-        in_specs=[pl.BlockSpec(memory_space=pltpu.SMEM)] + [pl.BlockSpec(memory_space=pl.ANY)] * 4,
+        in_specs=[pl.BlockSpec(memory_space=pl.ANY)] * 5,
         out_specs=(pl.BlockSpec(memory_space=pl.ANY),) * 2,
         scratch_shapes=[
+            pltpu.SMEM(doc_blocks.shape, jnp.int32),
             pltpu.VMEM((tokens * heads, width), bf16),
             pltpu.VMEM((tokens * heads, width), bf16),
             pltpu.VMEM((window, width), bf16),
@@ -345,7 +354,7 @@
             pltpu.VMEM((2, 5, 2 * BLOCK, width), bf16),
             pltpu.VMEM((n_head, tokens, width), bf16),
             pltpu.VMEM((tokens * heads, width), bf16),
-            dma((4,)),
+            dma((5,)),
             dma((5, 2)),
             dma((5, 2)),
             dma((2, 5, 2)),
@@ -355,15 +364,20 @@
             dma((n_head + 1,)),
         ],
         compiler_params=pltpu.CompilerParams(
-            collective_id=0, has_side_effects=True, vmem_limit_bytes=67043328
+            collective_id=0, has_side_effects=True, vmem_limit_bytes=48 * 1024 * 1024
         ),
         name="attention_backward",
     )(
-        doc_blocks,
-        flat(query_heads),
-        flat(out_grad),
-        jnp.transpose(key_head, (1, 0, 2)),
-        jnp.transpose(value_head, (1, 0, 2)),
+        *(
+            pltpu.with_memory_space_constraint(x, pltpu.HBM)
+            for x in (
+                doc_blocks,
+                flat(query_heads),
+                flat(out_grad),
+                jnp.transpose(key_head, (1, 0, 2)),
+                jnp.transpose(value_head, (1, 0, 2)),
+            )
+        )
     )
     kv = jnp.transpose(kv, (0, 2, 1, 3))
     return dq.reshape(tokens, heads, width), kv[0], kv[1]

time: 78.2 us -> 54.9 us (0.70)
  the two profiles are of different devices: /device:TPU:382 before, /device:TPU:30 now
where the time goes in v3:
time: 54.9 us; the launch traced here: 54.8 us
  Pallas kernels  52.5 us (96%)
  local copies, waits for them, and re-layouts  1.63 us (3%)
  between operations  0.64 us (1%)
    pallas_call x1, Pallas kernels, on_device(): pl.pallas_call(functools.partial(kernel, n_ctx, n_head, heads, doc_blocks...  52.5 us

profile of v3, /device:TPU:30, one launch (start us, length us, event | category | flops | bytes accessed | tf_op | source)
XLA Modules:
  0.0 54.8 jit_solution(14776537381629799692)
XLA Ops:
  0.6 52.5 %attention_backward.1 = (bf16[1024,128]{1,0:T(8,128)(2,1)S(1)}, bf16[2,6,256,128]{3,2,1,0:T(8,128)(2,1)S(1)}) custom-call(s32[32]{0:T(128)} %docs_hbm.1, bf16[1024,128]{1,0:T(8,128)(2,1)} %bitcast.14, bf16[1024,128]{1,0:T(8,128)(2,1)} %bitcast.15, bf16[6,256,128]{2,1,0:T(8,128)(2,1)} %bitcast.12, bf16[6,256,128]{2,1,0:T(8,128)(2,1)} %bitcast.13), custom_call_target="tpu_custom_call" | custom-call | tf_op jit(solution)/shard_map/attention_backward/pallas_call | solution.py:334
  53.1 0.9 %slice_bitcast_fusion = (bf16[256,6,128]{2,0,1:T(8,128)(2,1)}, bf16[256,6,128]{2,0,1:T(8,128)(2,1)}) fusion(bf16[2,256,6,128]{3,1,2,0:T(8,128)(2,1)S(1)} %bitcast.10), kind=kLoop, calls=%fused_computation | loop fusion | bytes 1572864 | tf_op jit(solution)/shard_map/squeeze | solution.py:383
  54.0 0.7 %copy.9 = bf16[256,4,128]{2,1,0:T(4,128)(2,1)} copy(bf16[256,4,128]{2,1,0:T(4,128)(2,1)S(1)} %bitcast.11) | data formatting | bytes 524288

commit v4 on v3

--- a/solution.py
+++ b/solution.py
@@ -28,8 +28,8 @@
     n_ctx, n_head, heads, docs,
     docs_hbm, q_hbm, do_hbm, k_hbm, v_hbm,
     dq_out, kv_out,
-    docs_ref, q_ref, do_ref, kw, vw, e_ref, dp_ref, stat, ds_ref, own, sb, rb, og, dq_ref,
-    load_sem, a_send, a_recv, b_send, b_recv, c_send, c_recv, out_sem,
+    docs_ref, q_ref, do_ref, kw, vw, e_ref, dp_ref, stat, ds_ref, own, hold, xs, xr, sums, rb, og, dq_ref,
+    load_sem, a_send, a_recv, x_send, x_recv, b_send, b_recv, c_send, c_recv, out_sem,
 ):
     width = q_ref.shape[1]
     shard = 2 * BLOCK
@@ -40,7 +40,6 @@
     h = lax.axis_index("head")
     role = lax.rem(h, 2)
     partner = h + 1 - 2 * role
-    other = lax.rem(h - 1 + 2 * role + n_head, n_head)
     group = h * heads // GROUP
 
     core = lax.rem(s, 2)
@@ -63,8 +62,8 @@
         copy.start()
 
     barrier = pltpu.get_barrier_semaphore()
-    peers = [(ctx(d), h) for d in range(-4, 5) if d != 0]
-    peers += [(ctx(d), partner) for d in range(-4, 5)] + [(s, other), (s, lax.rem(h + 2, n_head)), (s, lax.rem(h + n_head - 2, n_head))]
+    near_rows = [(s, lax.rem(h + n_head + d, n_head)) for d in (-2, -1, 1, 2)]
+    peers = [(ctx(-4), h), (ctx(-2), h), (sibling, h)] + near_rows
     for peer in peers:
         pl.semaphore_signal(barrier, inc=1, device_id=peer, device_id_type=MESH)
     pl.semaphore_wait(barrier, len(peers))
@@ -140,15 +139,17 @@
         back = 7 + qb - w
         q = q_ref[pl.ds(qb * rows, rows), :]
         do = do_ref[pl.ds(qb * rows, rows), :]
-        scores = dot(kw[pl.ds((w + 1) * BLOCK, BLOCK), :], q, NT)
-        if back == 0:
+        keys = pl.ds(pl.multiple_of((w + 1) * BLOCK, BLOCK), BLOCK)
+        scores = dot(kw[keys, :], q, NT)
+        if isinstance(w, int) and back == 0:
             scores = jnp.where(causal, scores, MASKED)
         top = jnp.max(scores, axis=0, keepdims=True) * to_log2
         e = jnp.exp2(scores * to_log2 - top)
-        dp = dot(vw[pl.ds((w + 1) * BLOCK, BLOCK), :], do, NT)
+        dp = dot(vw[keys, :], do, NT)
         at = w - qb
-        e_ref[qb, pl.ds(at * BLOCK, BLOCK), :] = e
-        dp_ref[qb, pl.ds(at * BLOCK, BLOCK), :] = dp
+        tile = pl.ds(pl.multiple_of(at * BLOCK, BLOCK), BLOCK)
+        e_ref[qb, tile, :] = e
+        dp_ref[qb, tile, :] = dp
         bias = jnp.where(back <= before[qb], jnp.float32(0), jnp.float32(MASKED))
         stat[qb, 0, pl.ds(at, 1), :] = top + bias
         stat[qb, 1, pl.ds(at, 1), :] = jnp.sum(e, axis=0, keepdims=True)
@@ -173,12 +174,12 @@
     for w in (3, 4):
         pair(0, w)
         pair(1, w)
-    for i in range(2):
-        across_far(i).wait_recv()
-        across_near(i).wait_recv()
-    for w in (1, 2, 5, 6):
-        pair(0, w)
-        pair(1, w)
+    for brought, first in ((across_far, 1 + 4 * core), (across_near, 5 - 4 * core)):
+        for i in range(2):
+            brought(i).wait_recv()
+        for w in (first, first + 1):
+            pair(0, w)
+            pair(1, w)
 
     factors, dots = [], []
     for qb in range(2):
@@ -187,9 +188,6 @@
         inv = 1.0 / jnp.sum(stat[qb, 1] * part, axis=0, keepdims=True)
         factors.append(part * inv)
         dots.append(jnp.sum(stat[qb, 2] * part, axis=0, keepdims=True) * inv)
-
-    back_sends = []
-    back_recv = {}
 
     def key_block(w):
         grads = [None, None]
@@ -205,30 +203,66 @@
                 dot(probs.astype(jnp.bfloat16), do_ref[pl.ds(qb * rows, rows), :], NN),
             )
             grads = [t if g is None else g + t for g, t in zip(grads, terms)]
-        grads[0] = grads[0] * scale
-        d, half = (8 - w) // 2, (w + 1) % 2
-        for i in range(2):
-            sb[w, i] = grads[i].astype(jnp.bfloat16)
-            if d == 0:
-                own[i, pl.ds(half * BLOCK, BLOCK), :] = grads[i]
-        for plane, row in enumerate((h, partner)):
-            if d == 0 and plane == 0:
-                continue
-            which = role if plane == 0 else 1 - role
-            copy = pltpu.make_async_remote_copy(
-                src_ref=sb.at[w, which],
-                dst_ref=rb.at[plane, d, pl.ds(half * BLOCK, BLOCK)],
-                send_sem=b_send.at[plane, d, half],
-                recv_sem=b_recv.at[plane, d, half],
-                device_id=(ctx(-d), row),
-                device_id_type=MESH,
-            )
-            copy.start()
-            back_sends.append(copy)
-            back_recv[plane, d, half] = copy
-
-    for w in (1, 3, 5, 7, 0, 2, 4, 6, 8):
-        key_block(w)
+        return grads[0] * scale, grads[1]
+
+    def across(i):
+        return pltpu.make_async_remote_copy(
+            src_ref=xs.at[i],
+            dst_ref=xr.at[i],
+            send_sem=x_send.at[i],
+            recv_sem=x_recv.at[i],
+            device_id=(sibling, h),
+            device_id_type=MESH,
+        )
+
+    def back(chips, half, plane):
+        which = role if plane == 0 else 1 - role
+        src = xr.at[0, which] if (chips, half) == (2, 0) else sums.at[chips, half, which]
+        return pltpu.make_async_remote_copy(
+            src_ref=src,
+            dst_ref=rb.at[plane, chips, pl.ds(half * BLOCK, BLOCK)],
+            send_sem=b_send.at[plane, chips, half],
+            recv_sem=b_recv.at[plane, chips, half],
+            device_id=(ctx(-2 * chips), h if plane == 0 else partner),
+            device_id_type=MESH,
+        )
+
+    for i, w in enumerate((1, 2, 5, 6)):
+        for kind, grad in enumerate(key_block(w)):
+            xs[i, kind] = grad.astype(jnp.bfloat16)
+        across(i).start()
+    for i, w in enumerate((0, 3, 4)):
+        for kind, grad in enumerate(key_block(w)):
+            hold[i, kind] = grad
+
+    def crossed(i, kind):
+        return xr[i, kind].astype(jnp.float32)
+
+    across(0).wait_recv()
+
+    @pl.when(core == 1)
+    def _():
+        for plane in range(2):
+            back(2, 0, plane).start()
+
+    across(1).wait_recv()
+    for kind in range(2):
+        sums[2, 1, kind] = (hold[0, kind] + jnp.where(core == 1, crossed(1, kind), 0.0)).astype(jnp.bfloat16)
+    for plane in range(2):
+        back(2, 1, plane).start()
+    across(2).wait_recv()
+    across(3).wait_recv()
+    for half in range(2):
+        for kind in range(2):
+            sums[1, half, kind] = (hold[1 + half, kind] + crossed(half + 2 * core, kind)).astype(jnp.bfloat16)
+        for plane in range(2):
+            back(1, half, plane).start()
+    for half in range(2):
+        for kind, grad in enumerate(key_block(7 + half)):
+            grad = grad + jnp.where(core == 0, crossed(2 + half, kind), 0.0)
+            own[kind, pl.ds(half * BLOCK, BLOCK), :] = grad
+            sums[0, half, kind] = grad.astype(jnp.bfloat16)
+        back(0, half, 1).start()
 
     for qb in range(2):
         grad = dot(kw[pl.ds((qb + 1) * BLOCK, REACH * BLOCK), :], ds_ref[qb], TN)
@@ -262,12 +296,17 @@
             if step <= steps(way, chunk):
                 hop(way, step, chunk).start()
 
+    @pl.when(core == 1)
+    def _():
+        for plane in range(2):
+            back(2, 0, plane).wait_recv()
+            own[role, pl.ds(0, BLOCK), :] += rb[plane, 2, pl.ds(0, BLOCK), :].astype(jnp.float32)
+
     for half in range(2):
         total = own[role, pl.ds(half * BLOCK, BLOCK), :]
-        for (plane, d, at), copy in back_recv.items():
-            if at == half:
-                copy.wait_recv()
-                total = total + rb[plane, d, pl.ds(half * BLOCK, BLOCK), :].astype(jnp.float32)
+        for chips, plane in ((0, 1), (1, 0), (1, 1)) + ((2, 0), (2, 1)) * half:
+            back(chips, half, plane).wait_recv()
+            total = total + rb[plane, chips, pl.ds(half * BLOCK, BLOCK), :].astype(jnp.float32)
         og[h, pl.ds(half * BLOCK, BLOCK), :] = total.astype(jnp.bfloat16)
         for chunk in range(half * CHUNKS // 2, (half + 1) * CHUNKS // 2):
             for way in range(2):
@@ -301,8 +340,11 @@
             arrive(far, way, chunk)
     put(row(far, 0), 2 * far - 1)
 
-    for copy in back_sends:
-        copy.wait_send()
+    for i in range(4):
+        across(i).wait_send()
+    for half in range(2):
+        for chips, plane in ((0, 1), (1, 0), (1, 1)) + ((2, 0), (2, 1)) * half:
+            back(chips, half, plane).wait_send()
     for i in range(2):
         far_half(i, 1).wait_send()
         near(i).wait_send()
@@ -313,6 +355,7 @@
     def _():
         for i in range(2):
             far_half(i, 0).wait_send()
+            back(2, 0, i).wait_send()
 
     for way in range(2):
         for chunk in range(CHUNKS):
@@ -320,6 +363,18 @@
                 hop(way, step, chunk).wait_send()
     dq_copy.wait()
     for copy in outs:
+        copy.wait()
+
+
+def copy_out(dq, kv, dq_out, dk_out, dv_out, sems):
+    copies = [
+        pltpu.make_async_copy(kv.at[0], dk_out, sems.at[0]),
+        pltpu.make_async_copy(kv.at[1], dv_out, sems.at[1]),
+        pltpu.make_async_copy(dq, dq_out, sems.at[2]),
+    ]
+    for copy in copies:
+        copy.start()
+    for copy in copies:
         copy.wait()
 
 
@@ -350,15 +405,20 @@
             pltpu.VMEM((2, 3, REACH, rows), f32),
             pltpu.VMEM((2, REACH * BLOCK, rows), bf16),
             pltpu.VMEM((2, 2 * BLOCK, width), f32),
-            pltpu.VMEM((REACH + 1, 2, BLOCK, width), bf16),
-            pltpu.VMEM((2, 5, 2 * BLOCK, width), bf16),
+            pltpu.VMEM((3, 2, BLOCK, width), f32),
+            pltpu.VMEM((4, 2, BLOCK, width), bf16),
+            pltpu.VMEM((4, 2, BLOCK, width), bf16),
+            pltpu.VMEM((3, 2, 2, BLOCK, width), bf16),
+            pltpu.VMEM((2, 3, 2 * BLOCK, width), bf16),
             pltpu.VMEM((n_head, tokens, width), bf16),
             pltpu.VMEM((tokens * heads, width), bf16),
             dma((5,)),
             dma((5, 2)),
             dma((5, 2)),
-            dma((2, 5, 2)),
-            dma((2, 5, 2)),
+            dma((4,)),
+            dma((4,)),
+            dma((2, 3, 2)),
+            dma((2, 3, 2)),
             dma((2, n_head // 2, CHUNKS)),
             dma((2, n_head // 2, CHUNKS)),
             dma((n_head + 1,)),
@@ -379,8 +439,25 @@
             )
         )
     )
-    kv = jnp.transpose(kv, (0, 2, 1, 3))
-    return dq.reshape(tokens, heads, width), kv[0], kv[1]
+    any_space = pl.BlockSpec(memory_space=pl.ANY)
+    dq, dk, dv = pl.pallas_call(
+        copy_out,
+        out_shape=(
+            jax.ShapeDtypeStruct(dq.shape, bf16),
+            jax.ShapeDtypeStruct(kv.shape[1:], bf16),
+            jax.ShapeDtypeStruct(kv.shape[1:], bf16),
+        ),
+        in_specs=[any_space] * 2,
+        out_specs=(any_space,) * 3,
+        scratch_shapes=[dma((3,))],
+        compiler_params=pltpu.CompilerParams(vmem_limit_bytes=8 * 1024 * 1024),
+        name="copy_out",
+    )(dq, kv)
+    return (
+        dq.reshape(tokens, heads, width),
+        jnp.transpose(dk, (1, 0, 2)),
+        jnp.transpose(dv, (1, 0, 2)),
+    )
 
 
 def solution(mesh):

time: 54.9 us -> 52.5 us (0.956)
  local copies, waits for them, and re-layouts: 1.63 us -> 0 us
  Pallas kernels: 52.5 us -> 51.8 us
    pallas_call x1, Pallas kernels: 52.5 us -> 50.8 us  [on_device(): pl.pallas_call(functools.partial(kernel, n_ctx, n_head, heads, doc_blocks...]
    pallas_call x0 -> x1, Pallas kernels: none -> 0.99 us  [on_device(): pl.pallas_call(copy_out, out_shape=(jax.ShapeDtypeStruct(dq.shape, bf16),...]
    squeeze x1 -> x0, local copies, waits for them, and re-layouts: 0.93 us -> none  [on_device(): return (dq.reshape(tokens, heads, width), kv[0], kv[1])]
    unnamed x1 -> x0, local copies, waits for them, and re-layouts: 0.7 us -> none
where the time goes in v4:
time: 52.5 us; the launch traced here: 52.4 us
  Pallas kernels  51.8 us (99%)
  between operations  0.64 us (1%)
    pallas_call x1, Pallas kernels, on_device(): pl.pallas_call(functools.partial(kernel, n_ctx, n_head, heads, doc_blocks...  50.8 us

profile of v4, /device:TPU:30, one launch (start us, length us, event | category | flops | bytes accessed | tf_op | source)
XLA Modules:
  0.0 52.4 jit_solution(17526561247781107587)
XLA Ops:
  0.6 50.8 %attention_backward.1 = (bf16[1024,128]{1,0:T(8,128)(2,1)S(1)}, bf16[2,6,256,128]{3,2,1,0:T(8,128)(2,1)S(1)}) custom-call(s32[32]{0:T(128)} %docs_hbm.1, bf16[1024,128]{1,0:T(8,128)(2,1)} %bitcast.9, bf16[1024,128]{1,0:T(8,128)(2,1)} %bitcast.10, bf16[6,256,128]{2,1,0:T(8,128)(2,1)} %bitcast.7, bf16[6,256,128]{2,1,0:T(8,128)(2,1)} %bitcast.8), custom_call_target="tpu_custom_call" | custom-call | tf_op jit(solution)/shard_map/attention_backward/pallas_call | solution.py:389
  51.4 1.0 %copy_out.1 = (bf16[1024,128]{1,0:T(8,128)(2,1)}, bf16[6,256,128]{2,1,0:T(8,128)(2,1)}, bf16[6,256,128]{2,1,0:T(8,128)(2,1)}) custom-call(bf16[1024,128]{1,0:T(8,128)(2,1)S(1)} %get-tuple-element.8.dq, bf16[2,6,256,128]{3,2,1,0:T(8,128)(2,1)S(1)} %get-tuple-element.9.kv), custom_call_target="tpu_custom_call" | custom-call | tf_op jit(solution)/shard_map/copy_out/pallas_call | solution.py:443

commit v5 on v4

--- a/solution.py
+++ b/solution.py
@@ -13,7 +13,8 @@
 MASKED = -1e30
 LOG2E = 1.4426950408889634
 MESH = pl.DeviceIdType.MESH
-CHUNKS = 4
+CHUNKS = 2
+RELAYS = (2, 4)
 
 NT = (((1,), (1,)), ((), ()))
 NN = (((1,), (0,)), ((), ()))
@@ -28,7 +29,7 @@
     n_ctx, n_head, heads, docs,
     docs_hbm, q_hbm, do_hbm, k_hbm, v_hbm,
     dq_out, kv_out,
-    docs_ref, q_ref, do_ref, kw, vw, e_ref, dp_ref, stat, ds_ref, own, hold, xs, xr, sums, rb, og, dq_ref,
+    docs_ref, q_ref, do_ref, kw, vw, e_ref, dp_ref, stat, ds_ref, own, hold, xs, xr, sums, rb, total_ref, dq_ref,
     load_sem, a_send, a_recv, x_send, x_recv, b_send, b_recv, c_send, c_recv, out_sem,
 ):
     width = q_ref.shape[1]
@@ -245,18 +246,22 @@
         for plane in range(2):
             back(2, 0, plane).start()
 
+    across(2).wait_recv()
+
+    def near_sum(half):
+        for kind in range(2):
+            sums[1, half, kind] = (hold[1 + half, kind] + crossed(half + 2 * core, kind)).astype(jnp.bfloat16)
+        for plane in range(2):
+            back(1, half, plane).start()
+
+    near_sum(0)
     across(1).wait_recv()
     for kind in range(2):
         sums[2, 1, kind] = (hold[0, kind] + jnp.where(core == 1, crossed(1, kind), 0.0)).astype(jnp.bfloat16)
     for plane in range(2):
         back(2, 1, plane).start()
-    across(2).wait_recv()
     across(3).wait_recv()
-    for half in range(2):
-        for kind in range(2):
-            sums[1, half, kind] = (hold[1 + half, kind] + crossed(half + 2 * core, kind)).astype(jnp.bfloat16)
-        for plane in range(2):
-            back(1, half, plane).start()
+    near_sum(1)
     for half in range(2):
         for kind, grad in enumerate(key_block(7 + half)):
             grad = grad + jnp.where(core == 0, crossed(2 + half, kind), 0.0)
@@ -267,7 +272,7 @@
     for qb in range(2):
         grad = dot(kw[pl.ds((qb + 1) * BLOCK, REACH * BLOCK), :], ds_ref[qb], TN)
         dq_ref[pl.ds(qb * rows, rows), :] = (jnp.transpose(grad) * scale).astype(jnp.bfloat16)
-    dq_copy = pltpu.make_async_copy(dq_ref, dq_out, out_sem.at[n_head])
+    dq_copy = pltpu.make_async_copy(dq_ref, dq_out, out_sem.at[0])
     dq_copy.start()
 
     piece = shard // CHUNKS
@@ -278,9 +283,10 @@
 
     def hop(way, step, chunk):
         relay = (step - 1) // 2 * 2
-        part = og.at[row(-relay, way), pl.ds(chunk * piece, piece)]
+        rows_of = pl.ds(chunk * piece, piece)
+        part = kv_out.at[row(-relay, way), rows_of]
         return pltpu.make_async_remote_copy(
-            src_ref=part,
+            src_ref=part if relay else total_ref.at[rows_of],
             dst_ref=part,
             send_sem=c_send.at[way, step - 1, chunk],
             recv_sem=c_recv.at[way, step - 1, chunk],
@@ -307,38 +313,23 @@
         for chips, plane in ((0, 1), (1, 0), (1, 1)) + ((2, 0), (2, 1)) * half:
             back(chips, half, plane).wait_recv()
             total = total + rb[plane, chips, pl.ds(half * BLOCK, BLOCK), :].astype(jnp.float32)
-        og[h, pl.ds(half * BLOCK, BLOCK), :] = total.astype(jnp.bfloat16)
+        total_ref[pl.ds(half * BLOCK, BLOCK), :] = total.astype(jnp.bfloat16)
         for chunk in range(half * CHUNKS // 2, (half + 1) * CHUNKS // 2):
             for way in range(2):
                 pass_on(0, way, chunk)
 
-    outs = []
-
-    def put(of, index):
-        copy = pltpu.make_async_copy(og.at[of], kv_out.at[lax.rem(of, 2), of // 2], out_sem.at[index])
-        copy.start()
-        outs.append(copy)
-
-    def arrive(step, way, chunk):
-        if step <= steps(way, chunk):
-            hop(way, step, chunk).wait_recv()
-
-    put(h, 0)
-    for step in (2, 4):
+    total_copy = pltpu.make_async_copy(total_ref, kv_out.at[h], out_sem.at[1])
+    total_copy.start()
+    for step in RELAYS:
         for chunk in range(CHUNKS):
             for way in range(2):
-                arrive(step, way, chunk)
+                hop(way, step, chunk).wait_recv()
                 pass_on(step, way, chunk)
-    for step in (2, 4, 1, 3, 5):
-        for way in range(2):
-            if step % 2:
-                for chunk in range(CHUNKS):
-                    arrive(step, way, chunk)
-            put(row(-step, way), 2 * step - 1 + way)
-    for chunk in range(CHUNKS):
-        for way in range(2):
-            arrive(far, way, chunk)
-    put(row(far, 0), 2 * far - 1)
+    for way in range(2):
+        for chunk in range(CHUNKS):
+            for step in range(1, steps(way, chunk) + 1):
+                if step not in RELAYS:
+                    hop(way, step, chunk).wait_recv()
 
     for i in range(4):
         across(i).wait_send()
@@ -362,14 +353,13 @@
             for step in range(1, steps(way, chunk) + 1):
                 hop(way, step, chunk).wait_send()
     dq_copy.wait()
-    for copy in outs:
-        copy.wait()
+    total_copy.wait()
 
 
 def copy_out(dq, kv, dq_out, dk_out, dv_out, sems):
     copies = [
-        pltpu.make_async_copy(kv.at[0], dk_out, sems.at[0]),
-        pltpu.make_async_copy(kv.at[1], dv_out, sems.at[1]),
+        pltpu.make_async_copy(kv.at[:, 0], dk_out, sems.at[0]),
+        pltpu.make_async_copy(kv.at[:, 1], dv_out, sems.at[1]),
         pltpu.make_async_copy(dq, dq_out, sems.at[2]),
     ]
     for copy in copies:
@@ -390,7 +380,7 @@
         functools.partial(kernel, n_ctx, n_head, heads, doc_blocks.shape[0]),
         out_shape=(
             jax.ShapeDtypeStruct((tokens * heads, width), bf16),
-            jax.ShapeDtypeStruct((2, kv_count, tokens, width), bf16),
+            jax.ShapeDtypeStruct((n_head, tokens, width), bf16),
         ),
         in_specs=[pl.BlockSpec(memory_space=pl.ANY)] * 5,
         out_specs=(pl.BlockSpec(memory_space=pl.ANY),) * 2,
@@ -410,7 +400,7 @@
             pltpu.VMEM((4, 2, BLOCK, width), bf16),
             pltpu.VMEM((3, 2, 2, BLOCK, width), bf16),
             pltpu.VMEM((2, 3, 2 * BLOCK, width), bf16),
-            pltpu.VMEM((n_head, tokens, width), bf16),
+            pltpu.VMEM((tokens, width), bf16),
             pltpu.VMEM((tokens * heads, width), bf16),
             dma((5,)),
             dma((5, 2)),
@@ -421,7 +411,7 @@
             dma((2, 3, 2)),
             dma((2, n_head // 2, CHUNKS)),
             dma((2, n_head // 2, CHUNKS)),
-            dma((n_head + 1,)),
+            dma((2,)),
         ],
         compiler_params=pltpu.CompilerParams(
             collective_id=0, has_side_effects=True, vmem_limit_bytes=48 * 1024 * 1024
@@ -444,15 +434,15 @@
         copy_out,
         out_shape=(
             jax.ShapeDtypeStruct(dq.shape, bf16),
-            jax.ShapeDtypeStruct(kv.shape[1:], bf16),
-            jax.ShapeDtypeStruct(kv.shape[1:], bf16),
+            jax.ShapeDtypeStruct((kv_count, tokens, width), bf16),
+            jax.ShapeDtypeStruct((kv_count, tokens, width), bf16),
         ),
         in_specs=[any_space] * 2,
         out_specs=(any_space,) * 3,
         scratch_shapes=[dma((3,))],
         compiler_params=pltpu.CompilerParams(vmem_limit_bytes=8 * 1024 * 1024),
         name="copy_out",
-    )(dq, kv)
+    )(dq, kv.reshape(kv_count, 2, tokens, width))
     return (
         dq.reshape(tokens, heads, width),
         jnp.transpose(dk, (1, 0, 2)),

time: 52.5 us -> 51.2 us (0.975)
  Pallas kernels: 51.8 us -> 50.4 us
    pallas_call x1, Pallas kernels: 50.8 us -> 49.4 us  [on_device(): pl.pallas_call(functools.partial(kernel, n_ctx, n_head, heads, doc_blocks...]
where the time goes in v5:
time: 51.2 us; the launch traced here: 51.1 us
  Pallas kernels  50.4 us (98%)
  between operations  0.64 us (1%)
    pallas_call x1, Pallas kernels, on_device(): pl.pallas_call(functools.partial(kernel, n_ctx, n_head, heads, doc_blocks...  49.4 us

profile of v5, /device:TPU:30, one launch (start us, length us, event | category | flops | bytes accessed | tf_op | source)
XLA Modules:
  0.0 51.1 jit_solution(2600281615967345359)
XLA Ops:
  0.6 49.4 %attention_backward.1 = (bf16[1024,128]{1,0:T(8,128)(2,1)S(1)}, bf16[12,256,128]{2,1,0:T(8,128)(2,1)S(1)}) custom-call(s32[32]{0:T(128)} %docs_hbm.1, bf16[1024,128]{1,0:T(8,128)(2,1)} %bitcast.11, bf16[1024,128]{1,0:T(8,128)(2,1)} %bitcast.12, bf16[6,256,128]{2,1,0:T(8,128)(2,1)} %bitcast.9, bf16[6,256,128]{2,1,0:T(8,128)(2,1)} %bitcast.10), custom_call_target="tpu_custom_call" | custom-call | tf_op jit(solution)/shard_map/attention_backward/pallas_call | solution.py:379
  50.1 1.0 %copy_out.1 = (bf16[1024,128]{1,0:T(8,128)(2,1)}, bf16[6,256,128]{2,1,0:T(8,128)(2,1)}, bf16[6,256,128]{2,1,0:T(8,128)(2,1)}) custom-call(bf16[1024,128]{1,0:T(8,128)(2,1)S(1)} %get-tuple-element.8.dq, bf16[6,2,256,128]{3,2,1,0:T(8,128)(2,1)S(1)} %bitcast.8), custom_call_target="tpu_custom_call" | custom-call | tf_op jit(solution)/shard_map/copy_out/pallas_call | solution.py:433
